TPU v7x, 32 devices: a whole 2x2x4 slice. The times are simulated.
32 devices in a mesh: fsdp: 8 (over z, x), rep: 4 (over y, core).
Axes of the slice: x: 2, y: 2, z: 4, core: 2. Of those that a mesh axis runs over, the one named last changes fastest.
Arguments:
- expert_base_rows: bfloat16 [4, 1536, 4096], P('rep', None, 'fsdp'), may hold values from -6 to 6
- factor_in: bfloat16 [4, 1536, 32], P('rep'), may hold values from -6 to 6
- factor_out: bfloat16 [4, 32, 4096], P('rep', None, 'fsdp'), may hold values from -0.29882812 to 0.29882812
- source_group: int32 [4], replicated, may hold values from 0 to 3
- tp_order: int32 [8], replicated, may hold values from 0 to 7, each once
Outputs:
- rollout_weights: bfloat16 [4, 4, 1536, 4096], P('rep', None, 'fsdp')
Inputs may be any that keep to these rules, and one draw needn't show every extreme that they name: source_group[k] is the replica index along rep whose expert fills bucket k; entries may repeat. tp_order is a permutation of the 8 row blocks.
All inputs are finite; a program needn't handle non-finite values.
Results may differ from a plain program's by a relative error of at most 0.001.
Values may be sent and summed in bfloat16 or wider, within the bound.
A program may use at most 64 MiB of HBM per device.

v0:
```python
import jax
import jax.numpy as jnp
from jax import lax
from jax.sharding import PartitionSpec as P

ADAPTER_SCALING = 2.0


def body(expert_base_rows, factor_in, factor_out, source_group, tp_order):
    shard_count = lax.axis_size("fsdp")
    hidden_size = expert_base_rows.shape[1]
    slice_rows = hidden_size // shard_count
    adapter_delta = jnp.dot(factor_in[0], factor_out[0], preferred_element_type=jnp.float32)
    merged_weight = (
        expert_base_rows[0].astype(jnp.float32) + ADAPTER_SCALING * adapter_delta
    ).astype(jnp.bfloat16)
    blocks = jnp.take(
        merged_weight.reshape(shard_count, slice_rows, merged_weight.shape[1]), tp_order, axis=0
    )
    bucket = lax.all_to_all(blocks, "fsdp", split_axis=0, concat_axis=2, tiled=True)[0]
    shards = lax.all_gather(bucket[None], "rep", axis=0, tiled=True)
    sending_replicas = jnp.arange(shards.shape[0], dtype=jnp.int32)
    onehot = (source_group[:, None] == sending_replicas[None, :]).astype(jnp.bfloat16)
    gathered = jnp.einsum("kn,nfd->kfd", onehot, shards, preferred_element_type=jnp.float32)
    return gathered.astype(jnp.bfloat16)[None]


def solution(mesh):
    placed = (P("rep", None, "fsdp"), P("rep", None, None), P("rep", None, "fsdp"), P(), P())
    return jax.shard_map(
        body, mesh=mesh, in_specs=placed, out_specs=P("rep", None, "fsdp", None), check_vma=False
    )
```

profile of v0, /device:TPU:0, one launch (start us, length us, event | category | flops | bytes accessed | tf_op | source)
XLA Modules:
  0.0 128.6 jit_solution(2037912174429082487)
XLA Ops:
  6.5 0.0 copy-start
  6.5 0.0 all-gather.2.cloned.1.call-start
  6.5 0.7 compare_and_fusion
  7.2 0.7 compare_select_fusion
  7.9 0.0 copy-done
  7.9 2.0 %fusion.5 = bf16[1536,512]{1,0:T(8,128)(2,1)S(1)} fusion(bf16[1,1536,512]{2,1,0:T(8,128)(2,1)} %param.5, bf16[1,1536,32]{1,2,0:T(8,128)(2,1)S(1)} %copy-done, bf16[1,32,512]{2,1,0:T(8,128)(2,1)} %param.7), kind=kOutput, calls=%fused_computation.6 | convolution fusion | flops 53477376 | bytes 3276800 | tf_op jit(solution)/shard_map/dot_general | solution.py:13
  9.9 0.6 gather_fusion
  10.6 0.2 broadcast_select_fusion
  10.8 44.1 %all_to_all.18 = bf16[8,192,512]{2,1,0:T(8,128)(2,1)S(1)} all-to-all(bf16[8,192,512]{2,1,0:T(8,128)(2,1)S(1)} %broadcast_select_fusion), channel_id=1, replica_groups=mesh['fsdp'=8,'rep'=4] {'fsdp'}, dimensions={0} | all-to-all | bytes 3145728 | tf_op jit(solution)/shard_map/all_to_all | solution.py:20
  54.9 1.3 %copy.16 = bf16[1,8,24,8,512]{4,3,1,2,0:T(8,128)(2,1)} copy(bf16[1,8,24,8,512]{4,3,2,1,0:T(8,128)(2,1)S(1)} %bitcast.21) | data formatting | bytes 3145728 | tf_op jit(solution)/shard_map/all_to_all | solution.py:20
  56.2 0.0 copy-start.1
  56.2 0.0 all-gather.2.cloned.1.call-update
  56.2 45.5 %all-gather.2.cloned.1.call-done = bf16[4,192,4096]{2,1,0:T(8,128)(2,1)} async-done(((bf16[1,192,4096]{2,1,0:T(8,128)(2,1)}), bf16[4,192,4096]{2,1,0:T(8,128)(2,1)}) %all-gather.2.cloned.1.call-update) | async-done | bytes 6291472 | tf_op jit(solution)/shard_map/all_gather | solution.py:21
  101.8 0.0 copy-done.1
  101.8 11.0 %fusion.1 = bf16[1,4,192,4096]{3,1,2,0:T(4,128)(2,1)} fusion(bf16[4,192,4096]{2,1,0:T(8,128)(2,1)} %all-gather.2.cloned.1.call-done, s32[4]{0:T(128)S(1)} %copy-done.1), kind=kOutput, calls=%fused_computation.3 | convolution fusion | flops 28311568 | bytes 12582928 | tf_op jit(solution)/shard_map/kn,nfd->kfd/dot_general | solution.py:24
  112.8 8.9 %copy.15 = bf16[1,4,192,4096]{3,2,1,0:T(8,128)(2,1)} copy(bf16[1,4,192,4096]{3,1,2,0:T(4,128)(2,1)} %fusion.1) | data formatting | bytes 12582912 | tf_op jit(solution)/shard_map/broadcast_in_dim | solution.py:25
  (1 shorter events, 0.0 us)
Async XLA Ops:
  6.5 1.4 %copy-start = (bf16[1,1536,32]{1,2,0:T(8,128)(2,1)S(1)}, bf16[1,1536,32]{1,2,0:T(8,128)(2,1)}, u32[]{:S(2)}) copy-start(bf16[1,1536,32]{1,2,0:T(8,128)(2,1)} %param.6) | copy-start | bytes 294916
  6.5 95.2 %all-gather.2.cloned.1.call-start = ((), (), s32[]{:S(2)}) async-start(), calls=%async_computation.1 | async-start | bytes 7864320 | tf_op jit(solution)/shard_map/all_gather | solution.py:21
  56.2 45.6 %copy-start.1 = (s32[4]{0:T(128)S(1)}, s32[4]{0:T(128)}, u32[]{:S(2)}) copy-start(s32[4]{0:T(128)} %param.8) | copy-start | bytes 52
Sparse Core Ops, SparseCore 0:
  56.3 45.3 all-gather.1
where the time goes:
time: 129 us
  waiting for transfers between devices  45.6 us (35%)
  blocking collectives  44.1 us (34%)
  between operations  13.4 us (10%)
  matrix products  13.1 us (10%)
  local copies, waits for them, and re-layouts  10.9 us (8%)
  other arithmetic  1.58 us (1%)
    all_gather x1, waiting for transfers between devices, body(): shards = lax.all_gather(bucket[None], 'rep', axis=0, tiled=True)  45.5 us
    all_to_all x1, blocking collectives, body(): lax.all_to_all(blocks, 'fsdp', split_axis=0, concat_axis=2, tiled=True)[0]  44.1 us
    dot_general x1, matrix products, body(): jnp.einsum('kn,nfd->kfd', onehot, shards, preferred_element_type=jnp.floa...  11 us
    broadcast_in_dim x1, local copies, waits for them, and re-layouts, body(): return gathered.astype(jnp.bfloat16)[None]  8.93 us
  transfers between devices with their start and end apart: 1, of which 1 were waited for; matrix products, arithmetic and copies ran while one was open for 0% of the time, Pallas kernels for 0%

commit v1 on v0

v1 whole, which is shorter than its diff:
```python
import functools

import jax
import jax.numpy as jnp
from jax import lax
from jax.experimental import pallas as pl
from jax.experimental.pallas import tpu as pltpu
from jax.sharding import PartitionSpec as P

ADAPTER_SCALING = 2.0
GRANT = 16 * 1024 * 1024
MESH = pl.DeviceIdType.MESH


def flipped(position, step):
    for bit in range(step.bit_length()):
        if (step >> bit) & 1:
            weight = 1 << bit
            position = position + weight * (1 - 2 * ((position // weight) % 2))
    return position


def target(position, step, count):
    return flipped(position, step) if count & (count - 1) == 0 else (position + step) % count


def origin(position, step, count):
    return flipped(position, step) if count & (count - 1) == 0 else (position + count - step) % count


def merge_kernel(count, order_ref, base_ref, left_ref, right_ref, out_ref, merged):
    me = lax.axis_index("fsdp")
    rows = base_ref.shape[0] // count
    delta = lax.dot_general(
        left_ref[...], right_ref[...], (((0,), (0,)), ((), ())), preferred_element_type=jnp.float32
    )
    merged[...] = (base_ref[...].astype(jnp.float32) + ADAPTER_SCALING * delta).astype(merged.dtype)
    for step in range(count):
        block = order_ref[target(me, step, count)]
        out_ref[step] = merged[pl.ds(pl.multiple_of(block * rows, rows), rows), :]


def exchange_kernel(count, replicas, cores, group, halves, x_ref, g_ref, *sems):
    own_sem, a_send, a_recv, y_send, y_recv, c_send, c_recv = sems
    me, rep = lax.axis_index("fsdp"), lax.axis_index("rep")
    chips = replicas // cores
    chip, core = rep // cores, rep % cores
    partner = chip * cores + (cores - 1 - core)
    rows = x_ref.shape[1] // halves
    groups = count // group
    pieces = groups * halves

    peers = [(target(me, s, count), rep) for s in range(1, count)]
    peers += [(me, ((chip + d) % chips) * cores + core) for d in range(1, chips)]
    if cores == 2:
        peers += [(me, partner)]
    barrier = pltpu.get_barrier_semaphore()
    for peer in peers:
        pl.semaphore_signal(barrier, inc=1, device_id=peer, device_id_type=MESH)
    pl.semaphore_wait(barrier, len(peers))

    def send(src, dst, send_sem, recv_sem, peer):
        return pltpu.make_async_remote_copy(
            src_ref=src, dst_ref=dst, send_sem=send_sem, recv_sem=recv_sem, device_id=peer, device_id_type=MESH
        )

    def part(half):
        return pl.ds(half * rows, rows)

    started = []
    arriving = {}
    keep = pltpu.make_async_copy(x_ref.at[0], g_ref.at[rep, 0], own_sem)
    keep.start()

    def exchange(step, half):
        copy = send(
            x_ref.at[step, part(half)], g_ref.at[rep, step, part(half)],
            a_send.at[step * halves + half], a_recv.at[step * halves + half],
            (target(me, step, count), rep),
        )
        copy.start()
        arriving[step, half] = copy

    def plane(index, number, half):
        return g_ref.at[index, pl.ds(number * group, group), part(half)]

    across = {}

    def forward(number, half):
        piece = number * halves + half
        own = group == 1 and number == 0
        src = x_ref.at[pl.ds(0, 1), part(half)] if own else plane(rep, number, half)
        dst = plane(rep, number, half)
        for d in range(1, chips):
            at = (d - 1) * pieces + piece
            copy = send(src, dst, y_send.at[at], y_recv.at[at], (me, ((chip + d) % chips) * cores + core))
            copy.start()
            across[d, number, half] = copy
        if cores == 2:
            copy = send(src, dst, c_send.at[piece], c_recv.at[piece], (me, partner))
            copy.start()
            started.append(copy)

    def relay(number, half):
        piece = number * halves + half
        for d in range(1, chips):
            across[d, number, half].wait_recv()
            if cores == 2:
                came = plane(((chip + chips - d) % chips) * cores + core, number, half)
                at = d * pieces + piece
                copy = send(came, came, c_send.at[at], c_recv.at[at], (me, partner))
                copy.start()
                started.append(copy)

    order = [(number, half) for number in range(groups) for half in range(halves)]
    lag = halves
    if group == 1:
        for half in range(halves):
            forward(0, half)
    for step in range(1, count):
        for half in range(halves):
            exchange(step, half)
    if group > 1:
        keep.wait()
    for at, (number, half) in enumerate(order):
        for step in range(max(1, number * group), (number + 1) * group):
            arriving[step, half].wait_recv()
        if group > 1 or number > 0:
            forward(number, half)
        if at >= lag:
            relay(*order[at - lag])
    for number, half in order[len(order) - lag:]:
        relay(number, half)
    for copy in started:
        copy.wait()
    for copy in across.values():
        copy.wait_send()
    for copy in arriving.values():
        copy.wait_send()
    if group == 1:
        keep.wait()


def select_kernel(count, source_ref, g_ref, out_ref, sems):
    me = lax.axis_index("fsdp")
    width = g_ref.shape[3]
    copies = []
    for bucket in range(out_ref.shape[0]):
        for step in range(count):
            columns = pl.ds(pl.multiple_of(origin(me, step, count) * width, width), width)
            copy = pltpu.make_async_copy(
                g_ref.at[source_ref[bucket], step], out_ref.at[bucket, :, columns], sems.at[bucket, step]
            )
            copy.start()
            copies.append(copy)
    for copy in copies:
        copy.wait()


def body(expert_base_rows, factor_in, factor_out, source_group, tp_order):
    count, replicas = lax.axis_size("fsdp"), lax.axis_size("rep")
    hidden, width = expert_base_rows.shape[1:]
    rows = hidden // count
    buckets = source_group.shape[0]
    cores = 2 if replicas % 2 == 0 else 1
    chips = replicas // cores
    group = max(1, count // 8) if count % 8 == 0 else 1
    halves = 2 if group == 1 and rows % 32 == 0 else 1
    pieces = count // group * halves
    vmem, smem, anywhere = (pl.BlockSpec(memory_space=m) for m in (pltpu.VMEM, pltpu.SMEM, pl.ANY))
    kind = expert_base_rows.dtype

    blocks = pl.pallas_call(
        functools.partial(merge_kernel, count),
        out_shape=pltpu.VMEM((count, rows, width), kind),
        in_specs=[smem, vmem, vmem, vmem],
        out_specs=vmem,
        scratch_shapes=[pltpu.VMEM((hidden, width), kind)],
        compiler_params=pltpu.CompilerParams(vmem_limit_bytes=GRANT),
        name="merge",
    )(tp_order, expert_base_rows[0], factor_in[0].T, factor_out[0])

    dma = pltpu.SemaphoreType.DMA
    planes = pl.pallas_call(
        functools.partial(exchange_kernel, count, replicas, cores, group, halves),
        out_shape=pltpu.VMEM((replicas, count, rows, width), kind),
        in_specs=[vmem],
        out_specs=vmem,
        scratch_shapes=[
            dma,
            dma((count * halves,)), dma((count * halves,)),
            dma((max(1, chips - 1) * pieces,)), dma((max(1, chips - 1) * pieces,)),
            dma((chips * pieces,)), dma((chips * pieces,)),
        ],
        compiler_params=pltpu.CompilerParams(collective_id=0, has_side_effects=True, vmem_limit_bytes=GRANT),
        name="exchange",
    )(blocks)

    out = pl.pallas_call(
        functools.partial(select_kernel, count),
        out_shape=jax.ShapeDtypeStruct((buckets, rows, count * width), kind),
        in_specs=[smem, vmem],
        out_specs=anywhere,
        scratch_shapes=[dma((buckets, count))],
        compiler_params=pltpu.CompilerParams(vmem_limit_bytes=GRANT),
        name="select",
    )(source_group, planes)
    return out[None]


def solution(mesh):
    placed = (P("rep", None, "fsdp"), P("rep", None, None), P("rep", None, "fsdp"), P(), P())
    return jax.shard_map(
        body, mesh=mesh, in_specs=placed, out_specs=P("rep", None, "fsdp", None), check_vma=False
    )
```

time: 129 us -> 56.1 us (0.43)
  Pallas kernels: 0 us -> 52 us
  waiting for transfers between devices: 45.6 us -> 0 us
  blocking collectives: 44.1 us -> 0 us
  between operations: 13.4 us -> 0.03 us
  matrix products: 13.1 us -> 0 us
  local copies, waits for them, and re-layouts: 10.9 us -> 3.73 us
  other arithmetic: 1.58 us -> 0 us
    pallas_call x0 -> x3, Pallas kernels: none -> 52 us  [the longest x1 47.4 us: body(): pl.pallas_call(functools.partial(exchange_kernel, count, replicas, cores,...]
    all_gather x1 -> x0, waiting for transfers between devices: 45.5 us -> none  [body(): shards = lax.all_gather(bucket[None], 'rep', axis=0, tiled=True)]
    all_to_all x1 -> x0, blocking collectives: 44.1 us -> none  [body(): lax.all_to_all(blocks, 'fsdp', split_axis=0, concat_axis=2, tiled=True)[0]]
    dot_general x2 -> x0, matrix products: 13.1 us -> none  [the longest x1 11 us: body(): jnp.einsum('kn,nfd->kfd', onehot, shards, preferred_element_type=jnp.floa...]
    broadcast_in_dim x1 -> x0, local copies, waits for them, and re-layouts: 8.93 us -> none  [body(): return gathered.astype(jnp.bfloat16)[None]]
    unnamed x4 -> x10, local copies, waits for them, and re-layouts: 0.01 us -> 3.73 us
    all_to_all x1 -> x0, local copies, waits for them, and re-layouts: 1.31 us -> none  [body(): lax.all_to_all(blocks, 'fsdp', split_axis=0, concat_axis=2, tiled=True)[0]]
  transfers between devices with their start and end apart: 1 -> 0, of which waited for: 1 -> 0; matrix products, arithmetic and copies ran while one was open for 0% -> 0% of each run, Pallas kernels for 0% -> 0%
where the time goes in v1:
time: 56.1 us; the launch traced here: 55.8 us
  Pallas kernels  52 us (93%)
  local copies, waits for them, and re-layouts  3.73 us (7%)
    pallas_call x1, Pallas kernels, body(): pl.pallas_call(functools.partial(exchange_kernel, count, replicas, cores,...  47.4 us
    unnamed x10, local copies, waits for them, and re-layouts  3.73 us
    pallas_call x1, Pallas kernels, body(): pl.pallas_call(functools.partial(select_kernel, count), out_shape=jax.Sha...  3.46 us
    pallas_call x1, Pallas kernels, body(): pl.pallas_call(functools.partial(merge_kernel, count), out_shape=pltpu.VM...  1.24 us

profile of v1, /device:TPU:0, one launch (start us, length us, event | category | flops | bytes accessed | tf_op | source)
XLA Modules:
  0.0 55.8 jit_solution(9779232692925498804)
XLA Ops:
  0.0 0.0 copy-start.3
  0.0 0.0 copy-start
  0.0 1.4 %copy-done = bf16[1,1536,512]{2,1,0:T(8,128)(2,1)S(1)} copy-done((bf16[1,1536,512]{2,1,0:T(8,128)(2,1)S(1)}, bf16[1,1536,512]{2,1,0:T(8,128)(2,1)}, u32[]{:S(2)}) %copy-start) | copy-done | bytes 1572888
  1.4 0.0 copy-start.1
  1.4 0.9 %copy-done.1 = bf16[1,1536,32]{1,2,0:T(8,128)(2,1)S(1)} copy-done((bf16[1,1536,32]{1,2,0:T(8,128)(2,1)S(1)}, bf16[1,1536,32]{1,2,0:T(8,128)(2,1)}, u32[]{:S(2)}) %copy-start.1) | copy-done | bytes 98328
  2.3 0.0 copy-start.2
  2.3 0.8 %copy-done.2 = bf16[1,32,512]{2,1,0:T(8,128)(2,1)S(1)} copy-done((bf16[1,32,512]{2,1,0:T(8,128)(2,1)S(1)}, bf16[1,32,512]{2,1,0:T(8,128)(2,1)}, u32[]{:S(2)}) %copy-start.2) | copy-done | bytes 32792
  3.1 0.0 copy-start.4
  3.1 0.7 %copy-done.4 = s32[8]{0:T(128)S(1)} copy-done((s32[8]{0:T(128)S(1)}, s32[8]{0:T(128)}, u32[]{:S(2)}) %copy-start.4) | copy-done | bytes 56
  3.7 1.2 %merge.1.x_ref = bf16[8,192,512]{2,1,0:T(8,128)(2,1)S(1)} custom-call(s32[8]{0:T(128)S(1)} %copy-done.4, bf16[1536,512]{1,0:T(8,128)(2,1)S(1)} %bitcast.6, bf16[32,1536]{1,0:T(8,128)(2,1)S(1)} %bitcast.7, bf16[32,512]{1,0:T(8,128)(2,1)S(1)} %bitcast.8), custom_call_target="tpu_custom_call" | custom-call | tf_op jit(solution)/shard_map/merge/pallas_call | solution.py:173
  5.0 47.4 %exchange.1.g_ref = bf16[4,8,192,512]{3,2,1,0:T(8,128)(2,1)S(1)} custom-call(bf16[8,192,512]{2,1,0:T(8,128)(2,1)S(1)} %merge.1.x_ref), custom_call_target="tpu_custom_call" | custom-call | tf_op jit(solution)/shard_map/exchange/pallas_call | solution.py:184
  52.3 0.0 copy-done.3
  52.3 3.5 %select.1 = bf16[4,192,4096]{2,1,0:T(8,128)(2,1)} custom-call(s32[4]{0:T(128)S(1)} %copy-done.3, bf16[4,8,192,512]{3,2,1,0:T(8,128)(2,1)S(1)} %exchange.1.g_ref), custom_call_target="tpu_custom_call" | custom-call | tf_op jit(solution)/shard_map/select/pallas_call | solution.py:199
Async XLA Ops:
  0.0 52.3 %copy-start.3 = (s32[4]{0:T(128)S(1)}, s32[4]{0:T(128)}, u32[]{:S(2)}) copy-start(s32[4]{0:T(128)} %source_ref.1) | copy-start | bytes 52
  0.0 1.4 %copy-start = (bf16[1,1536,512]{2,1,0:T(8,128)(2,1)S(1)}, bf16[1,1536,512]{2,1,0:T(8,128)(2,1)}, u32[]{:S(2)}) copy-start(bf16[1,1536,512]{2,1,0:T(8,128)(2,1)} %param.5) | copy-start | bytes 4718596
  1.4 0.9 %copy-start.1 = (bf16[1,1536,32]{1,2,0:T(8,128)(2,1)S(1)}, bf16[1,1536,32]{1,2,0:T(8,128)(2,1)}, u32[]{:S(2)}) copy-start(bf16[1,1536,32]{1,2,0:T(8,128)(2,1)} %param.6) | copy-start | bytes 294916
  2.3 0.8 %copy-start.2 = (bf16[1,32,512]{2,1,0:T(8,128)(2,1)S(1)}, bf16[1,32,512]{2,1,0:T(8,128)(2,1)}, u32[]{:S(2)}) copy-start(bf16[1,32,512]{2,1,0:T(8,128)(2,1)} %param.7) | copy-start | bytes 98308
  3.1 0.7 %copy-start.4 = (s32[8]{0:T(128)S(1)}, s32[8]{0:T(128)}, u32[]{:S(2)}) copy-start(s32[8]{0:T(128)} %order_ref.1) | copy-start | bytes 100

commit v2 on v1

--- a/solution.py
+++ b/solution.py
@@ -28,20 +28,19 @@
     return flipped(position, step) if count & (count - 1) == 0 else (position + count - step) % count
 
 
-def merge_kernel(count, order_ref, base_ref, left_ref, right_ref, out_ref, merged):
-    me = lax.axis_index("fsdp")
-    rows = base_ref.shape[0] // count
-    delta = lax.dot_general(
-        left_ref[...], right_ref[...], (((0,), (0,)), ((), ())), preferred_element_type=jnp.float32
-    )
-    merged[...] = (base_ref[...].astype(jnp.float32) + ADAPTER_SCALING * delta).astype(merged.dtype)
-    for step in range(count):
-        block = order_ref[target(me, step, count)]
-        out_ref[step] = merged[pl.ds(pl.multiple_of(block * rows, rows), rows), :]
-
-
-def exchange_kernel(count, replicas, cores, group, halves, x_ref, g_ref, *sems):
-    own_sem, a_send, a_recv, y_send, y_recv, c_send, c_recv = sems
+def exchange_kernel(
+    count, replicas, cores, group, halves,
+    order_in, base_in, left_in, right_in, g_ref, order_ref, base_ref, left_ref, right_ref, merged, x_ref, *sems
+):
+    load_sems, own_sem, a_send, a_recv, y_send, y_recv, c_send, c_recv = sems
+    loads = [
+        pltpu.make_async_copy(src, dst, load_sems.at[at])
+        for at, (src, dst) in enumerate(
+            ((left_in, left_ref), (right_in, right_ref), (order_in, order_ref), (base_in, base_ref))
+        )
+    ]
+    for load in loads:
+        load.start()
     me, rep = lax.axis_index("fsdp"), lax.axis_index("rep")
     chips = replicas // cores
     chip, core = rep // cores, rep % cores
@@ -57,6 +56,18 @@
     barrier = pltpu.get_barrier_semaphore()
     for peer in peers:
         pl.semaphore_signal(barrier, inc=1, device_id=peer, device_id_type=MESH)
+
+    loads[0].wait()
+    loads[1].wait()
+    delta = lax.dot_general(
+        left_ref[...], right_ref[...], (((0,), (0,)), ((), ())), preferred_element_type=jnp.float32
+    )
+    loads[2].wait()
+    loads[3].wait()
+    total = base_ref[...].astype(jnp.float32) + ADAPTER_SCALING * delta
+    merged[...] = total.astype(merged.dtype).reshape(merged.shape)
+    for step in range(count):
+        x_ref[step] = merged[order_ref[target(me, step, count)]]
     pl.semaphore_wait(barrier, len(peers))
 
     def send(src, dst, send_sem, recv_sem, peer):
@@ -167,34 +178,33 @@
     group = max(1, count // 8) if count % 8 == 0 else 1
     halves = 2 if group == 1 and rows % 32 == 0 else 1
     pieces = count // group * halves
-    vmem, smem, anywhere = (pl.BlockSpec(memory_space=m) for m in (pltpu.VMEM, pltpu.SMEM, pl.ANY))
+    vmem, smem, hbm, anywhere = (
+        pl.BlockSpec(memory_space=m) for m in (pltpu.VMEM, pltpu.SMEM, pltpu.HBM, pl.ANY)
+    )
     kind = expert_base_rows.dtype
 
-    blocks = pl.pallas_call(
-        functools.partial(merge_kernel, count),
-        out_shape=pltpu.VMEM((count, rows, width), kind),
-        in_specs=[smem, vmem, vmem, vmem],
-        out_specs=vmem,
-        scratch_shapes=[pltpu.VMEM((hidden, width), kind)],
-        compiler_params=pltpu.CompilerParams(vmem_limit_bytes=GRANT),
-        name="merge",
-    )(tp_order, expert_base_rows[0], factor_in[0].T, factor_out[0])
-
+    left, right = factor_in[0].T, factor_out[0]
     dma = pltpu.SemaphoreType.DMA
     planes = pl.pallas_call(
         functools.partial(exchange_kernel, count, replicas, cores, group, halves),
         out_shape=pltpu.VMEM((replicas, count, rows, width), kind),
-        in_specs=[vmem],
+        in_specs=[hbm] * 4,
         out_specs=vmem,
         scratch_shapes=[
-            dma,
+            pltpu.SMEM(tp_order.shape, tp_order.dtype),
+            pltpu.VMEM((hidden, width), kind),
+            pltpu.VMEM(left.shape, kind),
+            pltpu.VMEM(right.shape, kind),
+            pltpu.VMEM((count, rows, width), kind),
+            pltpu.VMEM((count, rows, width), kind),
+            dma((4,)), dma,
             dma((count * halves,)), dma((count * halves,)),
             dma((max(1, chips - 1) * pieces,)), dma((max(1, chips - 1) * pieces,)),
             dma((chips * pieces,)), dma((chips * pieces,)),
         ],
         compiler_params=pltpu.CompilerParams(collective_id=0, has_side_effects=True, vmem_limit_bytes=GRANT),
         name="exchange",
-    )(blocks)
+    )(*(pltpu.with_memory_space_constraint(a, pltpu.HBM) for a in (tp_order, expert_base_rows[0], left, right)))
 
     out = pl.pallas_call(
         functools.partial(select_kernel, count),

time: 56.1 us -> 51.4 us (0.916)
  local copies, waits for them, and re-layouts: 3.73 us -> 0.01 us
  Pallas kernels: 52 us -> 51.2 us
    unnamed x10 -> x2, local copies, waits for them, and re-layouts: 3.73 us -> 0.01 us
    pallas_call x1 -> x0, Pallas kernels: 1.24 us -> none  [body(): pl.pallas_call(functools.partial(merge_kernel, count), out_shape=pltpu.VM...]
where the time goes in v2:
time: 51.4 us; the launch traced here: 51.3 us
  Pallas kernels  51.2 us (100%)
    pallas_call x1, Pallas kernels, body(): pl.pallas_call(functools.partial(exchange_kernel, count, replicas, cores,...  47.8 us
    pallas_call x1, Pallas kernels, body(): pl.pallas_call(functools.partial(select_kernel, count), out_shape=jax.Sha...  3.46 us

profile of v2, /device:TPU:0, one launch (start us, length us, event | category | flops | bytes accessed | tf_op | source)
XLA Modules:
  0.0 51.3 jit_solution(5634319919684316133)
XLA Ops:
  0.0 0.0 copy-start
  0.0 47.8 %exchange.1.g_ref = bf16[4,8,192,512]{3,2,1,0:T(8,128)(2,1)S(1)} custom-call(s32[8]{0:T(128)} %order_in.1, bf16[1536,512]{1,0:T(8,128)(2,1)} %bitcast.6, bf16[32,1536]{1,0:T(8,128)(2,1)} %bitcast.7, bf16[32,512]{1,0:T(8,128)(2,1)} %bitcast.8), custom_call_target="tpu_custom_call" | custom-call | tf_op jit(solution)/shard_map/exchange/pallas_call | solution.py:188
  47.8 0.0 copy-done
  47.8 3.5 %select.1 = bf16[4,192,4096]{2,1,0:T(8,128)(2,1)} custom-call(s32[4]{0:T(128)S(1)} %copy-done, bf16[4,8,192,512]{3,2,1,0:T(8,128)(2,1)S(1)} %exchange.1.g_ref), custom_call_target="tpu_custom_call" | custom-call | tf_op jit(solution)/shard_map/select/pallas_call | solution.py:209
Async XLA Ops:
  0.0 47.8 %copy-start = (s32[4]{0:T(128)S(1)}, s32[4]{0:T(128)}, u32[]{:S(2)}) copy-start(s32[4]{0:T(128)} %source_ref.1) | copy-start | bytes 52

commit v3 on v2

v3 whole, which is shorter than its diff:
```python
import functools

import jax
import jax.numpy as jnp
from jax import lax
from jax.experimental import pallas as pl
from jax.experimental.pallas import tpu as pltpu
from jax.sharding import PartitionSpec as P

ADAPTER_SCALING = 2.0
GRANT = 40 * 1024 * 1024
MESH = pl.DeviceIdType.MESH


def flipped(position, step):
    for bit in range(step.bit_length()):
        if (step >> bit) & 1:
            weight = 1 << bit
            position = position + weight * (1 - 2 * ((position // weight) % 2))
    return position


def target(position, step, count):
    return flipped(position, step) if count & (count - 1) == 0 else (position + step) % count


def origin(position, step, count):
    return flipped(position, step) if count & (count - 1) == 0 else (position + count - step) % count


def exchange_kernel(
    count, replicas, cores, group, halves,
    source_in, order_in, base_in, left_in, right_in, out_ref,
    source_ref, order_ref, base_ref, left_ref, right_ref, merged, x_ref, *rest
):
    planes, sems = rest[: count // group], rest[count // group:]
    load_sems, own_sem, a_send, a_recv, y_send, y_recv, c_send, c_recv = sems
    loads = [
        pltpu.make_async_copy(src, dst, load_sems.at[at])
        for at, (src, dst) in enumerate(
            ((left_in, left_ref), (right_in, right_ref), (order_in, order_ref), (base_in, base_ref),
             (source_in, source_ref))
        )
    ]
    for load in loads:
        load.start()
    me, rep = lax.axis_index("fsdp"), lax.axis_index("rep")
    chips = replicas // cores
    chip, core = rep // cores, rep % cores
    partner = chip * cores + (cores - 1 - core)
    rows = x_ref.shape[1] // halves
    groups = count // group
    pieces = groups * halves

    peers = [(target(me, s, count), rep) for s in range(1, count)]
    peers += [(me, ((chip + d) % chips) * cores + core) for d in range(1, chips)]
    if cores == 2:
        peers += [(me, partner)]
    barrier = pltpu.get_barrier_semaphore()
    for peer in peers:
        pl.semaphore_signal(barrier, inc=1, device_id=peer, device_id_type=MESH)

    loads[0].wait()
    loads[1].wait()
    delta = lax.dot_general(
        left_ref[...], right_ref[...], (((0,), (0,)), ((), ())), preferred_element_type=jnp.float32
    )
    loads[2].wait()
    loads[3].wait()
    loads[4].wait()
    total = base_ref[...].astype(jnp.float32) + ADAPTER_SCALING * delta
    merged[...] = total.astype(merged.dtype).reshape(merged.shape)
    for step in range(count):
        x_ref[step] = merged[order_ref[target(me, step, count)]]
    pl.semaphore_wait(barrier, len(peers))

    def send(src, dst, send_sem, recv_sem, peer):
        return pltpu.make_async_remote_copy(
            src_ref=src, dst_ref=dst, send_sem=send_sem, recv_sem=recv_sem, device_id=peer, device_id_type=MESH
        )

    def part(half):
        return pl.ds(half * rows, rows)

    crossing = {}
    arriving = {}
    keep = pltpu.make_async_copy(x_ref.at[0], planes[0].at[rep, 0], own_sem)
    keep.start()

    def exchange(step, half):
        copy = send(
            x_ref.at[step, part(half)], planes[step // group].at[rep, step % group, part(half)],
            a_send.at[step * halves + half], a_recv.at[step * halves + half],
            (target(me, step, count), rep),
        )
        copy.start()
        arriving[step, half] = copy

    def plane(index, number, half):
        return planes[number].at[index, :, part(half)]

    across = {}

    def forward(number, half):
        piece = number * halves + half
        own = group == 1 and number == 0
        src = x_ref.at[pl.ds(0, 1), part(half)] if own else plane(rep, number, half)
        dst = plane(rep, number, half)
        for d in range(1, chips):
            at = (d - 1) * pieces + piece
            copy = send(src, dst, y_send.at[at], y_recv.at[at], (me, ((chip + d) % chips) * cores + core))
            copy.start()
            across[d, number, half] = copy
        if cores == 2:
            copy = send(src, dst, c_send.at[piece], c_recv.at[piece], (me, partner))
            copy.start()
            crossing[0, number, half] = copy

    def relay(number, half):
        piece = number * halves + half
        for d in range(1, chips):
            across[d, number, half].wait_recv()
            if cores == 2:
                came = plane(((chip + chips - d) % chips) * cores + core, number, half)
                at = d * pieces + piece
                copy = send(came, came, c_send.at[at], c_recv.at[at], (me, partner))
                copy.start()
                crossing[d, number, half] = copy

    def finish(number):
        if number == 0 and group == 1:
            keep.wait()
        if cores == 2:
            for d in range(chips):
                for half in range(halves):
                    crossing[d, number, half].wait_recv()
        width = x_ref.shape[2]
        for slot in range(group):
            first = pl.multiple_of(origin(me, number * group + slot, count) * width, width)
            for bucket in range(out_ref.shape[0]):
                out_ref[bucket, :, pl.ds(first, width)] = planes[number][source_ref[bucket], slot]

    order = [(number, half) for number in range(groups) for half in range(halves)]
    lag = 2 * halves
    if group == 1:
        for half in range(halves):
            forward(0, half)
    for step in range(1, count):
        for half in range(halves):
            exchange(step, half)
    if group > 1:
        keep.wait()
    for at in range(len(order) + 2 * lag):
        if at < len(order):
            number, half = order[at]
            for step in range(max(1, number * group), (number + 1) * group):
                arriving[step, half].wait_recv()
            if group > 1 or number > 0:
                forward(number, half)
        if 0 <= at - lag < len(order):
            relay(*order[at - lag])
        if 0 <= at - 2 * lag < len(order):
            number, half = order[at - 2 * lag]
            if half == halves - 1:
                finish(number)
    for copy in (*crossing.values(), *across.values(), *arriving.values()):
        copy.wait_send()


def body(expert_base_rows, factor_in, factor_out, source_group, tp_order):
    count, replicas = lax.axis_size("fsdp"), lax.axis_size("rep")
    hidden, width = expert_base_rows.shape[1:]
    rows = hidden // count
    cores = 2 if replicas % 2 == 0 else 1
    chips = replicas // cores
    group = max(1, count // 8) if count % 8 == 0 else 1
    halves = 2 if group == 1 and rows % 32 == 0 else 1
    pieces = count // group * halves
    kind = expert_base_rows.dtype

    left, right = factor_in[0].T, factor_out[0]
    dma = pltpu.SemaphoreType.DMA
    whole = functools.partial(pltpu.with_memory_space_constraint, memory_space=pltpu.HBM)
    out = pl.pallas_call(
        functools.partial(exchange_kernel, count, replicas, cores, group, halves),
        out_shape=pltpu.VMEM((source_group.shape[0], rows, count * width), kind),
        in_specs=[pl.BlockSpec(memory_space=pltpu.HBM)] * 5,
        out_specs=pl.BlockSpec(memory_space=pltpu.VMEM),
        scratch_shapes=[
            pltpu.SMEM(source_group.shape, source_group.dtype),
            pltpu.SMEM(tp_order.shape, tp_order.dtype),
            pltpu.VMEM((hidden, width), kind),
            pltpu.VMEM(left.shape, kind),
            pltpu.VMEM(right.shape, kind),
            pltpu.VMEM((count, rows, width), kind),
            pltpu.VMEM((count, rows, width), kind),
            *[pltpu.VMEM((replicas, group, rows, width), kind)] * (count // group),
            dma((5,)), dma,
            dma((count * halves,)), dma((count * halves,)),
            dma((max(1, chips - 1) * pieces,)), dma((max(1, chips - 1) * pieces,)),
            dma((chips * pieces,)), dma((chips * pieces,)),
        ],
        compiler_params=pltpu.CompilerParams(collective_id=0, has_side_effects=True, vmem_limit_bytes=GRANT),
        name="exchange",
    )(*map(whole, (source_group, tp_order, expert_base_rows[0], left, right)))
    return out[None]


def solution(mesh):
    placed = (P("rep", None, "fsdp"), P("rep", None, None), P("rep", None, "fsdp"), P(), P())
    return jax.shard_map(
        body, mesh=mesh, in_specs=placed, out_specs=P("rep", None, "fsdp", None), check_vma=False
    )
```

time: 51.4 us -> 50.6 us (0.984)
  Pallas kernels: 51.2 us -> 47.8 us
  local copies, waits for them, and re-layouts: 0.01 us -> 2.71 us
    pallas_call x1 -> x0, Pallas kernels: 3.46 us -> none  [body(): pl.pallas_call(functools.partial(select_kernel, count), out_shape=jax.Sha...]
    unnamed x2 -> x1, local copies, waits for them, and re-layouts: 0.01 us -> 2.71 us
where the time goes in v3:
time: 50.6 us; the launch traced here: 50.5 us
  Pallas kernels  47.8 us (94%)
  local copies, waits for them, and re-layouts  2.71 us (5%)
    pallas_call x1, Pallas kernels, body(): pl.pallas_call(functools.partial(exchange_kernel, count, replicas, cores,...  47.8 us
    unnamed x1, local copies, waits for them, and re-layouts  2.71 us

profile of v3, /device:TPU:0, one launch (start us, length us, event | category | flops | bytes accessed | tf_op | source)
XLA Modules:
  0.0 50.5 jit_solution(16660155074232270459)
XLA Ops:
  0.0 47.8 %exchange.1 = bf16[4,192,4096]{2,1,0:T(8,128)(2,1)S(1)} custom-call(s32[4]{0:T(128)} %source_in.1, s32[8]{0:T(128)} %order_in.1, bf16[1536,512]{1,0:T(8,128)(2,1)} %bitcast.7, bf16[32,1536]{1,0:T(8,128)(2,1)} %bitcast.8, bf16[32,512]{1,0:T(8,128)(2,1)} %bitcast.9), custom_call_target="tpu_custom_call" | custom-call | tf_op jit(solution)/shard_map/exchange/pallas_call | solution.py:184
  47.8 2.7 %copy.7 = bf16[1,4,192,4096]{3,2,1,0:T(8,128)(2,1)} copy(bf16[1,4,192,4096]{3,2,1,0:T(8,128)(2,1)S(1)} %bitcast.6) | data formatting | bytes 12582912
